TPU v7x, 32 devices: a whole 2x2x4 slice. The times are simulated.
32 devices in a mesh: lat: 4 (over y, x), lon: 8 (over z, core).
Axes of the slice: x: 2, y: 2, z: 4, core: 2. Of those that a mesh axis runs over, the one named last changes fastest.
Arguments:
- inputs: bfloat16 [360, 360, 256], P('lat', 'lon'), may hold values from -6 to 6
- kernel: bfloat16 [3, 3, 256, 256], replicated, may hold values from -0.125 to 0.125
- cotangent: bfloat16 [360, 360, 256], P('lat', 'lon'), may hold values from -6 to 6
Outputs:
- outputs: bfloat16 [360, 360, 256], P('lat', 'lon')
- input_grad: bfloat16 [360, 360, 256], P('lat', 'lon')
- kernel_grad: float32 [3, 3, 256, 256], replicated
All inputs are finite; a program needn't handle non-finite values.
Results may differ from a plain program's by a relative error of at most 0.001.
Values may be sent and summed in bfloat16 or wider, within the bound.
No kernel may reach another device: no remote copies, remote signals or barrier semaphores. Data moves between devices by JAX's collectives and lax.ppermute only.
A program may use at most 192 MiB of HBM per device.

v0:
```python
import math
import jax
import jax.numpy as jnp
from jax import lax
from jax.sharding import PartitionSpec as P


def with_halo(cells, sides, width):
    for axis, dim in sides:
        count = lax.axis_size(axis)
        head = lax.slice_in_dim(cells, 0, width, axis=dim)
        tail = lax.slice_in_dim(cells, cells.shape[dim] - width, cells.shape[dim], axis=dim)
        cells = jnp.concatenate(
            [
                lax.ppermute(tail, axis, [(i, (i + 1) % count) for i in range(count)]),
                cells,
                lax.ppermute(head, axis, [((i + 1) % count, i) for i in range(count)]),
            ],
            axis=dim,
        )
    return cells


def from_behind(value, axis, steps):
    count = lax.axis_size(axis)
    pairs = [(source, (source + steps) % count) for source in range(count)]
    return lax.ppermute(value, axis, pairs)


def patches(padded, rows, cols):
    pieces = [
        padded[row_tap : row_tap + rows, col_tap : col_tap + cols]
        for row_tap in range(3)
        for col_tap in range(3)
    ]
    return jnp.concatenate(pieces, axis=-1).reshape(rows * cols, -1)


def surround(field):
    return with_halo(field, (("lat", 0), ("lon", 1)), 1)


def polar(padded):
    both = jnp.stack([padded[1], padded[-2]])
    moved = from_behind(both, "lon", lax.axis_size("lon") // 2)
    return (moved[0], moved[1])


def edge_term(row_data, weights, cols, width):
    stacked = jnp.concatenate([row_data[offset : offset + cols] for offset in range(3)], axis=-1)
    return jnp.dot(stacked, weights.reshape(-1, width), preferred_element_type=jnp.float32)


def local(inputs, kernel, cotangent):
    rows, cols, width = inputs.shape
    north = lax.axis_index("lat") == 0
    south = lax.axis_index("lat") == lax.axis_size("lat") - 1
    padded = surround(inputs)
    top, bottom = polar(padded)
    padded = jnp.concatenate(
        [
            jnp.where(north, top, padded[0])[None],
            padded[1:-1],
            jnp.where(south, bottom, padded[-1])[None],
        ],
        0,
    )
    columns = patches(padded, rows, cols)
    outputs = jnp.dot(columns, kernel.reshape(-1, width), preferred_element_type=jnp.float32)
    outputs = outputs.reshape(rows, cols, width).astype(jnp.bfloat16)
    flat_grad = cotangent.reshape(-1, width)
    local_grad = lax.dot_general(
        columns, flat_grad, (((0,), (0,)), ((), ())), preferred_element_type=jnp.float32
    )
    local_grad = local_grad.reshape(3, 3, width, width)
    padded_grad = surround(cotangent)
    grad_top, grad_bottom = polar(padded_grad)
    empty_row = jnp.zeros_like(padded_grad[0])
    padded_grad = jnp.concatenate(
        [
            jnp.where(north, empty_row, padded_grad[0])[None],
            padded_grad[1:-1],
            jnp.where(south, empty_row, padded_grad[-1])[None],
        ],
        0,
    )
    flipped = jnp.transpose(kernel[::-1, ::-1], (0, 1, 3, 2))
    input_grad = jnp.dot(
        patches(padded_grad, rows, cols),
        flipped.reshape(-1, width),
        preferred_element_type=jnp.float32,
    )
    input_grad = input_grad.reshape(rows, cols, width)
    north_term = edge_term(grad_top, flipped[2], cols, width)
    south_term = edge_term(grad_bottom, flipped[0], cols, width)
    input_grad = input_grad.at[0].add(jnp.where(north, north_term, 0.0))
    input_grad = input_grad.at[-1].add(jnp.where(south, south_term, 0.0))
    factor = 1.0 / math.sqrt(rows * cols * lax.axis_size("lat") * lax.axis_size("lon"))
    partial_sum = lax.psum(local_grad, "lon")
    summed = lax.psum(partial_sum, "lat")
    return (outputs, input_grad.astype(jnp.bfloat16), summed * factor)


def solution(mesh):
    in_specs = (P("lat", "lon", None), P(), P("lat", "lon", None))
    out_specs = (P("lat", "lon", None), P("lat", "lon", None), P())
    return jax.shard_map(local, mesh=mesh, in_specs=in_specs, out_specs=out_specs, check_vma=False)
```

profile of v0, /device:TPU:0, one launch (start us, length us, event | category | flops | bytes accessed | tf_op | source)
XLA Modules:
  0.0 271.3 jit_solution(15557798716294932809)
XLA Ops:
  8.0 3.9 %collective-permute-start.1 = (bf16[1,45,256]{2,1,0:T(8,128)(2,1)S(1)}, bf16[1,45,256]{2,1,0:T(8,128)(2,1)S(1)}, u32[]{:S(2)}, u32[]{:S(2)}) collective-permute-start(bf16[1,45,256]{2,1,0:T(8,128)(2,1)S(1)} %get-tuple-element.37), channel_id=1, source_target_pairs={{8,0},{16,8},{24,16},{0,24},{9,1},{17,9},{25,17},{1,25},{10,2},{18... | collective-permute-start | bytes 69128 | tf_op jit(solution)/shard_map/ppermute | solution.py:17
  13.3 2.9 %collective-permute-start.6 = (bf16[1,45,256]{2,1,0:T(8,128)(2,1)}, bf16[1,45,256]{2,1,0:T(8,128)(2,1)S(1)}, u32[]{:S(2)}, u32[]{:S(2)}) collective-permute-start(bf16[1,45,256]{2,1,0:T(8,128)(2,1)} %get-tuple-element.35), channel_id=1, source_target_pairs={{8,0},{16,8},{24,16},{0,24},{9,1},{17,9},{25,17},{1,25},{10,2},{18... | collective-permute-start | bytes 69128 | tf_op jit(solution)/shard_map/ppermute | solution.py:17
  19.9 1.9 reshape.103
  22.2 3.5 %collective-permute-start.8 = (bf16[92,1,256]{2,1,0:T(2,128)(2,1)S(1)}, bf16[92,1,256]{2,1,0:T(2,128)(2,1)S(1)}, u32[]{:S(2)}, u32[]{:S(2)}) collective-permute-start(bf16[92,1,256]{2,1,0:T(2,128)(2,1)S(1)} %get-tuple-element.32), channel_id=1, source_target_pairs={{1,0},{2,1},{3,2},{4,3},{5,4},{6,5},{7,6},{0,7},{9,8},{10,9},{11,1... | collective-permute-start | bytes 141320 | tf_op jit(solution)/shard_map/ppermute | solution.py:17
  26.2 3.5 %collective-permute-start.3 = (bf16[92,1,256]{2,1,0:T(2,128)(2,1)S(1)}, bf16[92,1,256]{2,1,0:T(2,128)(2,1)S(1)}, u32[]{:S(2)}, u32[]{:S(2)}) collective-permute-start(bf16[92,1,256]{2,1,0:T(2,128)(2,1)S(1)} %get-tuple-element.34), channel_id=1, source_target_pairs={{1,0},{2,1},{3,2},{4,3},{5,4},{6,5},{7,6},{0,7},{9,8},{10,9},{11,1... | collective-permute-start | bytes 141320 | tf_op jit(solution)/shard_map/ppermute | solution.py:17
  29.8 2.6 collective-permute-done.2
  34.6 1.6 fusion.7
  36.2 2.8 %fusion.5 = bf16[90,45,2304]{2,1,0:T(8,128)(2,1)} fusion(bf16[90,45,2304]{2,1,0:T(8,128)(2,1)} %fusion.7, bf16[1,47,256]{2,1,0:T(8,128)(2,1)S(1)} %get-tuple-element.30, bf16[90,47,256]{2,1,0:T(8,128)(2,1)S(1)} %slice.295), kind=kLoop, calls=%fused_computation.15 | loop fusion | flops 4147200 | bytes 4401664
  40.7 1.7 fusion.15
  42.5 2.7 %fusion.13 = bf16[90,45,2304]{2,1,0:T(8,128)(2,1)} fusion(bf16[90,45,2304]{2,1,0:T(8,128)(2,1)} %fusion.15, bf16[1,47,256]{2,1,0:T(8,128)(2,1)S(1)} %get-tuple-element.28, bf16[90,47,256]{2,1,0:T(8,128)(2,1)S(1)} %slice.283), kind=kLoop, calls=%fused_computation.23 | loop fusion | flops 4147200 | bytes 4401664
  45.2 2.8 %fusion.23 = bf16[90,45,2304]{2,1,0:T(8,128)(2,1)} fusion(bf16[90,45,2304]{2,1,0:T(8,128)(2,1)} %fusion.13, bf16[90,47,256]{2,1,0:T(8,128)(2,1)S(1)} %slice.283, bf16[1,47,256]{2,1,0:T(8,128)(2,1)S(1)} %get-tuple-element.28), kind=kLoop, calls=%fused_computation.41 | loop fusion | flops 4147200 | bytes 4401664
  48.0 2.9 %fusion.22 = bf16[90,45,2304]{2,1,0:T(8,128)(2,1)} fusion(bf16[90,45,2304]{2,1,0:T(8,128)(2,1)} %fusion.23, bf16[92,45,256]{2,1,0:T(8,128)(2,1)S(1)} %constant_dynamic-update-slice_fusion, bf16[92,1,256]{2,1,0:T(2,128)(2,1)S(1)} %collective-permute-done.2), kind=kLoop, calls=%fused_computation.39 | loop fusion | flops 4147200 | bytes 4378624
  50.8 1.7 constant_dynamic-update-slice_fusion.3
  52.5 3.1 %fusion.21 = bf16[90,45,2304]{2,1,0:T(8,128)(2,1)} fusion(bf16[90,45,2304]{2,1,0:T(8,128)(2,1)} %constant_dynamic-update-slice_fusion.3, bf16[92,1,256]{2,1,0:T(2,128)(2,1)S(1)} %collective-permute-done.3, bf16[92,45,256]{2,1,0:T(8,128)(2,1)S(1)} %constant_dynamic-update-slice_fusion), kind=kLoop, calls=%fused_computation.37 | loop fusion | flops 4147200 | bytes 4378624
  55.6 1.7 fusion.11
  57.3 2.8 %fusion.9 = bf16[90,45,2304]{2,1,0:T(8,128)(2,1)} fusion(bf16[90,45,2304]{2,1,0:T(8,128)(2,1)} %fusion.11, bf16[1,47,256]{2,1,0:T(8,128)(2,1)S(1)} %get-tuple-element.27, bf16[90,47,256]{2,1,0:T(8,128)(2,1)S(1)} %slice.283), kind=kLoop, calls=%fused_computation.19 | loop fusion | flops 4147200 | bytes 4401664
  60.0 3.1 %fusion.20 = bf16[90,45,2304]{2,1,0:T(8,128)(2,1)} fusion(bf16[90,45,2304]{2,1,0:T(8,128)(2,1)} %fusion.9, bf16[1,47,256]{2,1,0:T(8,128)(2,1)S(1)} %get-tuple-element.27, bf16[90,47,256]{2,1,0:T(8,128)(2,1)S(1)} %slice.283), kind=kLoop, calls=%fused_computation.35 | loop fusion | flops 4147200 | bytes 4401664 | tf_op jit(solution)/shard_map/concatenate | solution.py:36
  63.2 19.5 %reshape.99 = bf16[4050,2304]{1,0:T(8,128)(2,1)} reshape(bf16[90,45,2304]{2,1,0:T(8,128)(2,1)} %fusion.20) | data formatting | bytes 37324800 | tf_op jit(solution)/shard_map/reshape | solution.py:36
  82.7 23.0 %copy.7 = bf16[4050,2304]{0,1:T(8,128)(2,1)} copy(bf16[4050,2304]{1,0:T(8,128)(2,1)} %reshape.99) | data formatting | bytes 37324800 | tf_op jit(solution)/shard_map/reshape | solution.py:36
  105.7 10.6 %fusion.24 = f32[3,3,256,256]{3,2,1,0:T(8,128)} fusion(bf16[3,3,256,4050]{3,2,1,0:T(8,128)(2,1)} %bitcast.46, bf16[4050,256,1,1]{1,0,2,3:T(8,128)(2,1)} %reshape.103), kind=kOutput, calls=%fused_computation.42 | convolution fusion | flops 4777574400 | bytes 23095296 | tf_op jit(solution)/shard_map/dot_general | solution.py:72
  116.4 2.7 fusion.19
  119.1 2.8 %fusion.18 = bf16[90,45,2304]{2,1,0:T(8,128)(2,1)} fusion(bf16[90,45,2304]{2,1,0:T(8,128)(2,1)} %fusion.19, bf16[92,45,256]{2,1,0:T(8,128)(2,1)S(1)} %copy-done.1, bf16[92,1,256]{2,1,0:T(2,128)(2,1)S(1)} %collective-permute-done.7), kind=kLoop, calls=%fused_computation.31 | loop fusion | flops 4147200 | bytes 4378624
  121.9 1.6 constant_dynamic-update-slice_fusion.7
  123.4 2.9 %fusion.17 = bf16[90,45,2304]{2,1,0:T(8,128)(2,1)} fusion(bf16[90,45,2304]{2,1,0:T(8,128)(2,1)} %constant_dynamic-update-slice_fusion.7, bf16[92,1,256]{2,1,0:T(2,128)(2,1)S(1)} %collective-permute-done.8, bf16[92,45,256]{2,1,0:T(8,128)(2,1)S(1)} %copy-done.1), kind=kLoop, calls=%fused_computation.29 | loop fusion | flops 4147200 | bytes 4378624
  127.9 2.7 %fusion.1 = bf16[90,45,2304]{2,1,0:T(8,128)(2,1)} fusion(bf16[90,45,2304]{2,1,0:T(8,128)(2,1)} %fusion.3, bf16[1,47,256]{2,1,0:T(8,128)(2,1)S(1)} %get-tuple-element.29, bf16[90,47,256]{2,1,0:T(8,128)(2,1)S(1)} %slice.295), kind=kLoop, calls=%fused_computation.11 | loop fusion | flops 4147200 | bytes 4401664
  130.7 2.7 fusion.16
  133.4 51.7 %all-reduce.3.cloned.1.call-done = f32[3,3,256,256]{3,2,1,0:T(8,128)} async-done(((f32[3,3,256,256]{3,2,1,0:T(8,128)}), f32[3,3,256,256]{3,2,1,0:T(8,128)}) %all-reduce.3.cloned.1.call-update) | async-done | bytes 2359312 | tf_op jit(solution)/shard_map/psum | solution.py:99
  185.2 9.9 %fusion.72 = f32[90,45,256]{2,1,0:T(8,128)S(1)} fusion(bf16[90,45,2304]{2,1,0:T(8,128)(2,1)} %fusion.16, bf16[2304,256,1]{1,0,2:T(8,128)(2,1)S(1)} %bitcast.50), kind=kOutput, calls=%fused_computation.114 | convolution fusion | flops 4777574400 | bytes 23989248 | tf_op jit(solution)/shard_map/dot_general | solution.py:88
  195.6 1.6 convert_element_type.7
  197.2 11.6 %convolution_convert_fusion = bf16[90,45,256]{2,1,0:T(8,128)(2,1)} fusion(bf16[90,45,2304]{2,1,0:T(8,128)(2,1)} %fusion.20, bf16[2304,256,1]{1,0,2:T(8,128)(2,1)S(1)} %bitcast.49), kind=kOutput, calls=%fused_computation.44 | convolution fusion | flops 4778611200 | bytes 21915648 | tf_op jit(solution)/shard_map/dot_general | solution.py:69
  208.8 52.4 %all-reduce.5.cloned.1.call-done = f32[3,3,256,256]{3,2,1,0:T(8,128)} async-done(((f32[3,3,256,256]{3,2,1,0:T(8,128)}), f32[3,3,256,256]{3,2,1,0:T(8,128)}) %all-reduce.5.cloned.1.call-update) | async-done | bytes 2359312 | tf_op jit(solution)/shard_map/psum | solution.py:100
  261.2 3.3 %broadcast_multiply_fusion = f32[3,3,256,256]{3,2,1,0:T(8,128)} fusion(f32[3,3,256,256]{3,2,1,0:T(8,128)} %all-reduce.5.cloned.1.call-done), kind=kLoop, calls=%fused_computation.45 | loop fusion | flops 589824 | bytes 4718592 | tf_op jit(solution)/shard_map/mul | solution.py:101
  (63 shorter events, 12.7 us)
Async XLA Ops:
  7.2 178.0 %all-reduce.3.cloned.1.call-start = ((), (), s32[]{:S(2)}) async-start(), calls=%async_computation | async-start | bytes 4718592 | tf_op jit(solution)/shard_map/psum | solution.py:99
  8.0 18.0 %collective-permute-start.1 = (bf16[1,45,256]{2,1,0:T(8,128)(2,1)S(1)}, bf16[1,45,256]{2,1,0:T(8,128)(2,1)S(1)}, u32[]{:S(2)}, u32[]{:S(2)}) collective-permute-start(bf16[1,45,256]{2,1,0:T(8,128)(2,1)S(1)} %get-tuple-element.37), channel_id=1, source_target_pairs={{8,0},{16,8},{24,16},{0,24},{9,1},{17,9},{25,17},{1,25},{10,2},{18... | collective-permute-start | bytes 69128 | tf_op jit(solution)/shard_map/ppermute | solution.py:17
  11.9 13.9 %collective-permute-start = (bf16[1,45,256]{2,1,0:T(8,128)(2,1)S(1)}, bf16[1,45,256]{2,1,0:T(8,128)(2,1)S(1)}, u32[]{:S(2)}, u32[]{:S(2)}) collective-permute-start(bf16[1,45,256]{2,1,0:T(8,128)(2,1)S(1)} %get-tuple-element.38), channel_id=1, source_target_pairs={{0,8},{8,16},{16,24},{24,0},{1,9},{9,17},{17,25},{25,1},{2,10},{10... | collective-permute-start | bytes 69128 | tf_op jit(solution)/shard_map/ppermute | solution.py:15
  13.3 8.7 %collective-permute-start.6 = (bf16[1,45,256]{2,1,0:T(8,128)(2,1)}, bf16[1,45,256]{2,1,0:T(8,128)(2,1)S(1)}, u32[]{:S(2)}, u32[]{:S(2)}) collective-permute-start(bf16[1,45,256]{2,1,0:T(8,128)(2,1)} %get-tuple-element.35), channel_id=1, source_target_pairs={{8,0},{16,8},{24,16},{0,24},{9,1},{17,9},{25,17},{1,25},{10,2},{18... | collective-permute-start | bytes 69128 | tf_op jit(solution)/shard_map/ppermute | solution.py:17
  16.2 5.6 %collective-permute-start.5 = (bf16[1,45,256]{2,1,0:T(8,128)(2,1)}, bf16[1,45,256]{2,1,0:T(8,128)(2,1)S(1)}, u32[]{:S(2)}, u32[]{:S(2)}) collective-permute-start(bf16[1,45,256]{2,1,0:T(8,128)(2,1)} %get-tuple-element.36), channel_id=1, source_target_pairs={{0,8},{8,16},{16,24},{24,0},{1,9},{9,17},{17,25},{25,1},{2,10},{10... | collective-permute-start | bytes 69128 | tf_op jit(solution)/shard_map/ppermute | solution.py:15
  17.9 2.0 copy-start.2
  21.8 4.0 %copy-start.4 = (bf16[90,45,256]{2,1,0:T(8,128)(2,1)S(1)}, bf16[90,45,256]{2,1,0:T(8,128)(2,1)}, u32[]{:S(2)}) copy-start(bf16[90,45,256]{2,1,0:T(8,128)(2,1)} %param.7) | copy-start | bytes 6220804
  22.0 12.5 %copy-start = (bf16[92,45,256]{2,1,0:T(8,128)(2,1)}, bf16[92,45,256]{2,1,0:T(8,128)(2,1)S(1)}, u32[]{:S(2)}) copy-start(bf16[92,45,256]{2,1,0:T(8,128)(2,1)S(1)} %constant_dynamic-update-slice_fusion.4) | copy-start | bytes 6359044
  22.2 7.5 %collective-permute-start.7 = (bf16[92,1,256]{2,1,0:T(2,128)(2,1)S(1)}, bf16[92,1,256]{2,1,0:T(2,128)(2,1)S(1)}, u32[]{:S(2)}, u32[]{:S(2)}) collective-permute-start(bf16[92,1,256]{2,1,0:T(2,128)(2,1)S(1)} %get-tuple-element.31), channel_id=1, source_target_pairs={{0,1},{1,2},{2,3},{3,4},{4,5},{5,6},{6,7},{7,0},{8,9},{9,10},{10,1... | collective-permute-start | bytes 141320 | tf_op jit(solution)/shard_map/ppermute | solution.py:15
  22.2 7.5 %collective-permute-start.8 = (bf16[92,1,256]{2,1,0:T(2,128)(2,1)S(1)}, bf16[92,1,256]{2,1,0:T(2,128)(2,1)S(1)}, u32[]{:S(2)}, u32[]{:S(2)}) collective-permute-start(bf16[92,1,256]{2,1,0:T(2,128)(2,1)S(1)} %get-tuple-element.32), channel_id=1, source_target_pairs={{1,0},{2,1},{3,2},{4,3},{5,4},{6,5},{7,6},{0,7},{9,8},{10,9},{11,1... | collective-permute-start | bytes 141320 | tf_op jit(solution)/shard_map/ppermute | solution.py:17
  26.1 6.3 %collective-permute-start.2 = (bf16[92,1,256]{2,1,0:T(2,128)(2,1)S(1)}, bf16[92,1,256]{2,1,0:T(2,128)(2,1)S(1)}, u32[]{:S(2)}, u32[]{:S(2)}) collective-permute-start(bf16[92,1,256]{2,1,0:T(2,128)(2,1)S(1)} %get-tuple-element.33), channel_id=1, source_target_pairs={{0,1},{1,2},{2,3},{3,4},{4,5},{5,6},{6,7},{7,0},{8,9},{9,10},{10,1... | collective-permute-start | bytes 141320 | tf_op jit(solution)/shard_map/ppermute | solution.py:15
  26.2 6.2 %collective-permute-start.3 = (bf16[92,1,256]{2,1,0:T(2,128)(2,1)S(1)}, bf16[92,1,256]{2,1,0:T(2,128)(2,1)S(1)}, u32[]{:S(2)}, u32[]{:S(2)}) collective-permute-start(bf16[92,1,256]{2,1,0:T(2,128)(2,1)S(1)} %get-tuple-element.34), channel_id=1, source_target_pairs={{1,0},{2,1},{3,2},{4,3},{5,4},{6,5},{7,6},{0,7},{9,8},{10,9},{11,1... | collective-permute-start | bytes 141320 | tf_op jit(solution)/shard_map/ppermute | solution.py:17
  29.8 165.3 %collective-permute-start.9 = (bf16[2,47,256]{2,1,0:T(8,128)(2,1)S(1)}, bf16[2,47,256]{2,1,0:T(8,128)(2,1)S(1)}, u32[]{:S(2)}, u32[]{:S(2)}) collective-permute-start(bf16[2,47,256]{2,1,0:T(8,128)(2,1)S(1)} %fusion.57), channel_id=1, source_target_pairs={{0,4},{1,5},{2,6},{3,7},{4,0},{5,1},{6,2},{7,3},{8,12},{9,13},{10,... | collective-permute-start | bytes 144392 | tf_op jit(solution)/shard_map/ppermute | solution.py:27
  32.4 8.3 %collective-permute-start.4 = (bf16[2,47,256]{2,1,0:T(8,128)(2,1)S(1)}, bf16[2,47,256]{2,1,0:T(8,128)(2,1)S(1)}, u32[]{:S(2)}, u32[]{:S(2)}) collective-permute-start(bf16[2,47,256]{2,1,0:T(8,128)(2,1)S(1)} %fusion.54), channel_id=1, source_target_pairs={{0,4},{1,5},{2,6},{3,7},{4,0},{5,1},{6,2},{7,3},{8,12},{9,13},{10,... | collective-permute-start | bytes 144392 | tf_op jit(solution)/shard_map/ppermute | solution.py:27
  116.3 144.9 %all-reduce.5.cloned.1.call-start = ((), (), s32[]{:S(2)}) async-start(), calls=%async_computation.1 | async-start | bytes 4718592 | tf_op jit(solution)/shard_map/psum | solution.py:100
  116.4 2.7 %copy-start.1 = (bf16[92,45,256]{2,1,0:T(8,128)(2,1)S(1)}, bf16[92,45,256]{2,1,0:T(8,128)(2,1)}, u32[]{:S(2)}) copy-start(bf16[92,45,256]{2,1,0:T(8,128)(2,1)} %copy-done) | copy-start | bytes 6359044
  119.1 2.8 %copy-start.3 = (bf16[90,45,256]{2,1,0:T(8,128)(2,1)S(1)}, bf16[90,45,256]{2,1,0:T(8,128)(2,1)}, u32[]{:S(2)}) copy-start(bf16[90,45,256]{2,1,0:T(8,128)(2,1)} %param.9) | copy-start | bytes 6220804
  133.4 51.8 %copy-start.8 = (bf16[3,3,256,256]{2,3,1,0:T(8,128)(2,1)S(1)}, bf16[3,3,256,256]{2,3,1,0:T(8,128)(2,1)}, u32[]{:S(2)}) copy-start(bf16[3,3,256,256]{2,3,1,0:T(8,128)(2,1)} %rev.3) | copy-start | bytes 3538948
  185.2 9.9 %copy-start.6 = (bf16[1,3,256,256]{3,2,1,0:T(8,128)(2,1)S(1)}, bf16[1,3,256,256]{3,2,1,0:T(8,128)(2,1)}, u32[]{:S(2)}) copy-start(bf16[1,3,256,256]{3,2,1,0:T(8,128)(2,1)} %get-tuple-element.40) | copy-start | bytes 1179652
  185.2 10.2 %copy-start.5 = (bf16[1,3,256,256]{3,2,1,0:T(8,128)(2,1)S(1)}, bf16[1,3,256,256]{3,2,1,0:T(8,128)(2,1)}, u32[]{:S(2)}) copy-start(bf16[1,3,256,256]{3,2,1,0:T(8,128)(2,1)} %get-tuple-element.39) | copy-start | bytes 1179652
  195.5 1.6 copy-start.7
Sparse Core Ops, SparseCore 0:
  116.4 68.6 all-reduce.2
  188.3 72.8 all-reduce.4
where the time goes:
time: 272 us; the launch traced here: 271 us
  waiting for transfers between devices  107 us (39%)
  local copies, waits for them, and re-layouts  54.5 us (20%)
  other arithmetic  48.6 us (18%)
  matrix products  32.5 us (12%)
  starting transfers between devices  14.6 us (5%)
  between operations  14.3 us (5%)
    psum x1, waiting for transfers between devices, local(): summed = lax.psum(partial_sum, 'lat')  52.4 us
    psum x1, waiting for transfers between devices, local(): partial_sum = lax.psum(local_grad, 'lon')  51.7 us
    reshape x2, local copies, waits for them, and re-layouts, patches(): return jnp.concatenate(pieces, axis=-1).reshape(rows * cols, -1)  42.5 us
    unnamed x14, other arithmetic  34.7 us
    ppermute x4, starting transfers between devices, with_halo(): lax.ppermute(head, axis, [((i + 1) % count, i) for i in range(count)])  13.9 us
    dot_general x1, matrix products, local(): jnp.dot(columns, kernel.reshape(-1, width), preferred_element_type=jnp.fl...  11.6 us
    dot_general x1, matrix products, local(): lax.dot_general(columns, flat_grad, (((0,), (0,)), ((), ())), preferred_e...  10.6 us
    dot_general x1, matrix products, local(): jnp.dot(patches(padded_grad, rows, cols), flipped.reshape(-1, width), pre...  9.87 us
  transfers between devices with their start and end apart: 12, of which 3 were waited for; matrix products, arithmetic and copies ran while one was open for 48% of the time, Pallas kernels for 0%

commit v1 on v0

--- a/solution.py
+++ b/solution.py
@@ -96,7 +96,7 @@
     input_grad = input_grad.at[0].add(jnp.where(north, north_term, 0.0))
     input_grad = input_grad.at[-1].add(jnp.where(south, south_term, 0.0))
     factor = 1.0 / math.sqrt(rows * cols * lax.axis_size("lat") * lax.axis_size("lon"))
-    partial_sum = lax.psum(local_grad, "lon")
+    partial_sum = jnp.sum(lax.all_gather(local_grad, "lon"), axis=0)
     summed = lax.psum(partial_sum, "lat")
     return (outputs, input_grad.astype(jnp.bfloat16), summed * factor)
 

time: 272 us -> 369 us (1.36)
  waiting for transfers between devices: 107 us -> 178 us
  other arithmetic: 48.6 us -> 60.8 us
  local copies, waits for them, and re-layouts: 54.5 us -> 62 us
  starting transfers between devices: 14.6 us -> 20 us
    all_gather x0 -> x1, waiting for transfers between devices: none -> 121 us  [local(): partial_sum = jnp.sum(lax.all_gather(local_grad, 'lon'), axis=0)]
    psum x1 -> x0, waiting for transfers between devices: 51.7 us -> none  [local(): partial_sum = lax.psum(local_grad, 'lon')]
    reduce_sum x0 -> x1, other arithmetic: none -> 9.35 us  [local(): partial_sum = jnp.sum(lax.all_gather(local_grad, 'lon'), axis=0)]
    psum x1, waiting for transfers between devices: 52.4 us -> 45.9 us  [local(): summed = lax.psum(partial_sum, 'lat')]
    ppermute x4, waiting for transfers between devices: 2.58 us -> 9.04 us  [with_halo(): lax.ppermute(tail, axis, [(i, (i + 1) % count) for i in range(count)])]
    ppermute x2, starting transfers between devices: 0.48 us -> 6.79 us  [from_behind(): return lax.ppermute(value, axis, pairs)]
    unnamed x25 -> x23, local copies, waits for them, and re-layouts: 5.17 us -> 9.12 us
    ppermute x4, starting transfers between devices: 13.9 us -> 9.99 us  [with_halo(): lax.ppermute(head, axis, [((i + 1) % count, i) for i in range(count)])]
  transfers between devices with their start and end apart: 12 -> 12, of which waited for: 3 -> 6; matrix products, arithmetic and copies ran while one was open for 48% -> 20% of each run, Pallas kernels for 0% -> 0%
where the time goes in v1:
time: 369 us; the launch traced here: 368 us
  waiting for transfers between devices  178 us (48%)
  local copies, waits for them, and re-layouts  62 us (17%)
  other arithmetic  60.8 us (16%)
  matrix products  32.8 us (9%)
  starting transfers between devices  20 us (5%)
  between operations  14.2 us (4%)
    all_gather x1, waiting for transfers between devices, local(): partial_sum = jnp.sum(lax.all_gather(local_grad, 'lon'), axis=0)  121 us
    psum x1, waiting for transfers between devices, local(): summed = lax.psum(partial_sum, 'lat')  45.9 us
    reshape x2, local copies, waits for them, and re-layouts, patches(): return jnp.concatenate(pieces, axis=-1).reshape(rows * cols, -1)  43.8 us
    unnamed x14, other arithmetic  35.7 us
    dot_general x1, matrix products, local(): jnp.dot(columns, kernel.reshape(-1, width), preferred_element_type=jnp.fl...  11.6 us
    dot_general x1, matrix products, local(): jnp.dot(patches(padded_grad, rows, cols), flipped.reshape(-1, width), pre...  10.5 us
    dot_general x1, matrix products, local(): lax.dot_general(columns, flat_grad, (((0,), (0,)), ((), ())), preferred_e...  10.4 us
    ppermute x4, starting transfers between devices, with_halo(): lax.ppermute(head, axis, [((i + 1) % count, i) for i in range(count)])  9.99 us
  transfers between devices with their start and end apart: 12, of which 6 were waited for; matrix products, arithmetic and copies ran while one was open for 20% of the time, Pallas kernels for 0%

profile of v1, /device:TPU:0, one launch (start us, length us, event | category | flops | bytes accessed | tf_op | source)
XLA Modules:
  0.0 367.8 jit_solution(15508358272657188416)
XLA Ops:
  8.0 3.0 collective-permute-start
  15.7 3.5 collective-permute-start.3
  19.2 4.0 %reshape.109 = bf16[4050,256,1,1]{1,0,2,3:T(8,128)(2,1)} reshape(bf16[90,45,256]{2,1,0:T(8,128)(2,1)} %param.9) | data formatting | bytes 4147200 | tf_op jit(solution)/shard_map/reshape | solution.py:71
  26.4 2.3 collective-permute-done.4
  30.4 2.8 fusion.13
  33.2 2.8 fusion.23
  36.0 2.9 fusion.22
  40.6 2.9 fusion.21
  45.3 2.9 fusion.9
  48.2 2.7 fusion.20
  50.9 19.3 %reshape.103 = bf16[4050,2304]{1,0:T(8,128)(2,1)} reshape(bf16[90,45,2304]{2,1,0:T(8,128)(2,1)} %fusion.20) | data formatting | bytes 37324800 | tf_op jit(solution)/shard_map/reshape | solution.py:36
  70.3 24.5 %copy.10 = bf16[4050,2304]{0,1:T(8,128)(2,1)} copy(bf16[4050,2304]{1,0:T(8,128)(2,1)} %reshape.103) | data formatting | bytes 37324800 | tf_op jit(solution)/shard_map/reshape | solution.py:36
  94.7 10.4 %fusion.24 = f32[3,3,256,256]{3,2,1,0:T(8,128)} fusion(bf16[3,3,256,4050]{3,2,1,0:T(8,128)(2,1)} %bitcast.48, bf16[4050,256,1,1]{1,0,2,3:T(8,128)(2,1)S(1)} %copy-done.2), kind=kOutput, calls=%fused_computation.42 | convolution fusion | flops 4777574400 | bytes 23095296 | tf_op jit(solution)/shard_map/dot_general | solution.py:72
  106.0 1.9 collective-permute-start.6
  108.9 3.8 %collective-permute-done.5 = bf16[1,45,256]{2,1,0:T(8,128)(2,1)S(1)} collective-permute-done((bf16[1,45,256]{2,1,0:T(8,128)(2,1)S(1)}, bf16[1,45,256]{2,1,0:T(8,128)(2,1)S(1)}, u32[]{:S(2)}, u32[]{:S(2)}) %collective-permute-start.5) | collective-permute-done | bytes 23072 | tf_op jit(solution)/shard_map/ppermute | solution.py:15
  112.7 2.1 constant_dynamic-update-slice_fusion.5
  115.7 3.5 collective-permute-start.8
  121.3 3.5 collective-permute-done.7
  125.4 5.3 %collective-permute-start.9 = (bf16[2,47,256]{2,1,0:T(8,128)(2,1)S(1)}, bf16[2,47,256]{2,1,0:T(8,128)(2,1)S(1)}, u32[]{:S(2)}, u32[]{:S(2)}) collective-permute-start(bf16[2,47,256]{2,1,0:T(8,128)(2,1)S(1)} %fusion.57), channel_id=1, source_target_pairs={{0,4},{1,5},{2,6},{3,7},{4,0},{5,1},{6,2},{7,3},{8,12},{9,13},{10,... | collective-permute-start | bytes 144392 | tf_op jit(solution)/shard_map/ppermute | solution.py:27
  130.8 2.3 pad_maximum_fusion.1
  135.5 2.7 fusion.5
  138.3 2.8 fusion.19
  141.0 3.6 fusion.18
  146.2 2.9 fusion.17
  150.7 2.7 fusion.1
  153.5 2.8 fusion.16
  156.3 120.8 %all-gather.3.cloned.1.call-done = f32[24,3,256,256]{3,2,1,0:T(8,128)} async-done(((f32[3,3,256,256]{3,2,1,0:T(8,128)}), f32[24,3,256,256]{3,2,1,0:T(8,128)}) %all-gather.3.cloned.1.call-update) | async-done | bytes 18874384 | tf_op jit(solution)/shard_map/all_gather | solution.py:99
  277.0 9.3 %reduce_sum.9 = f32[3,3,256,256]{3,2,1,0:T(8,128)} reduce(f32[8,3,3,256,256]{4,3,2,1,0:T(8,128)} %bitcast.47, f32[]{:T(128)} %constant.66.clone.1), dimensions={0}, to_apply=%region_0.1 | reduce | flops 4128768 | bytes 21233668 | tf_op jit(solution)/shard_map/reduce_sum | solution.py:99
  287.7 10.5 %fusion.72 = f32[90,45,256]{2,1,0:T(8,128)S(1)} fusion(bf16[90,45,2304]{2,1,0:T(8,128)(2,1)} %fusion.16, bf16[2304,256,1]{1,0,2:T(8,128)(2,1)S(1)} %bitcast.52), kind=kOutput, calls=%fused_computation.114 | convolution fusion | flops 4777574400 | bytes 23989248 | tf_op jit(solution)/shard_map/dot_general | solution.py:88
  300.2 11.6 %convolution_convert_fusion = bf16[90,45,256]{2,1,0:T(8,128)(2,1)} fusion(bf16[90,45,2304]{2,1,0:T(8,128)(2,1)} %fusion.20, bf16[2304,256,1]{1,0,2:T(8,128)(2,1)S(1)} %bitcast.51), kind=kOutput, calls=%fused_computation.44 | convolution fusion | flops 4778611200 | bytes 21915648 | tf_op jit(solution)/shard_map/dot_general | solution.py:69
  311.8 45.9 %all-reduce.2.cloned.1.call-done = f32[3,3,256,256]{3,2,1,0:T(8,128)} async-done(((f32[3,3,256,256]{3,2,1,0:T(8,128)}), f32[3,3,256,256]{3,2,1,0:T(8,128)}) %all-reduce.2.cloned.1.call-update) | async-done | bytes 2359312 | tf_op jit(solution)/shard_map/psum | solution.py:100
  357.7 3.3 broadcast_multiply_fusion
  (62 shorter events, 28.1 us)
Async XLA Ops:
  7.2 269.9 %all-gather.3.cloned.1.call-start = ((), (), s32[]{:S(2)}) async-start(), calls=%async_computation.1 | async-start | bytes 21233664 | tf_op jit(solution)/shard_map/all_gather | solution.py:99
  8.0 5.7 %collective-permute-start = (bf16[1,45,256]{2,1,0:T(8,128)(2,1)S(1)}, bf16[1,45,256]{2,1,0:T(8,128)(2,1)S(1)}, u32[]{:S(2)}, u32[]{:S(2)}) collective-permute-start(bf16[1,45,256]{2,1,0:T(8,128)(2,1)S(1)} %get-tuple-element.38), channel_id=1, source_target_pairs={{0,8},{8,16},{16,24},{24,0},{1,9},{9,17},{17,25},{25,1},{2,10},{10... | collective-permute-start | bytes 69128 | tf_op jit(solution)/shard_map/ppermute | solution.py:15
  10.9 4.5 %collective-permute-start.1 = (bf16[1,45,256]{2,1,0:T(8,128)(2,1)S(1)}, bf16[1,45,256]{2,1,0:T(8,128)(2,1)S(1)}, u32[]{:S(2)}, u32[]{:S(2)}) collective-permute-start(bf16[1,45,256]{2,1,0:T(8,128)(2,1)S(1)} %get-tuple-element.37), channel_id=1, source_target_pairs={{8,0},{16,8},{24,16},{0,24},{9,1},{17,9},{25,17},{1,25},{10,2},{18... | collective-permute-start | bytes 69128 | tf_op jit(solution)/shard_map/ppermute | solution.py:17
  15.7 7.6 %collective-permute-start.2 = (bf16[92,1,256]{2,1,0:T(2,128)(2,1)S(1)}, bf16[92,1,256]{2,1,0:T(2,128)(2,1)S(1)}, u32[]{:S(2)}, u32[]{:S(2)}) collective-permute-start(bf16[92,1,256]{2,1,0:T(2,128)(2,1)S(1)} %get-tuple-element.33), channel_id=1, source_target_pairs={{0,1},{1,2},{2,3},{3,4},{4,5},{5,6},{6,7},{7,0},{8,9},{9,10},{10,1... | collective-permute-start | bytes 141320 | tf_op jit(solution)/shard_map/ppermute | solution.py:15
  15.7 7.5 %collective-permute-start.3 = (bf16[92,1,256]{2,1,0:T(2,128)(2,1)S(1)}, bf16[92,1,256]{2,1,0:T(2,128)(2,1)S(1)}, u32[]{:S(2)}, u32[]{:S(2)}) collective-permute-start(bf16[92,1,256]{2,1,0:T(2,128)(2,1)S(1)} %get-tuple-element.34), channel_id=1, source_target_pairs={{1,0},{2,1},{3,2},{4,3},{5,4},{6,5},{7,6},{0,7},{9,8},{10,9},{11,1... | collective-permute-start | bytes 141320 | tf_op jit(solution)/shard_map/ppermute | solution.py:17
  23.3 5.4 %collective-permute-start.4 = (bf16[2,47,256]{2,1,0:T(8,128)(2,1)S(1)}, bf16[2,47,256]{2,1,0:T(8,128)(2,1)S(1)}, u32[]{:S(2)}, u32[]{:S(2)}) collective-permute-start(bf16[2,47,256]{2,1,0:T(8,128)(2,1)S(1)} %fusion.54), channel_id=1, source_target_pairs={{0,4},{1,5},{2,6},{3,7},{4,0},{5,1},{6,2},{7,3},{8,12},{9,13},{10,... | collective-permute-start | bytes 144392 | tf_op jit(solution)/shard_map/ppermute | solution.py:27
  36.0 2.9 copy-start.1
  70.3 24.5 %copy-start.2 = (bf16[4050,256,1,1]{1,0,2,3:T(8,128)(2,1)S(1)}, bf16[4050,256,1,1]{1,0,2,3:T(8,128)(2,1)}, u32[]{:S(2)}) copy-start(bf16[4050,256,1,1]{1,0,2,3:T(8,128)(2,1)} %reshape.109) | copy-start | bytes 6220804
  105.1 2.9 copy-start.5
  105.1 252.6 %all-reduce.2.cloned.1.call-start = ((), (), s32[]{:S(2)}) async-start(), calls=%async_computation | async-start | bytes 4718592 | tf_op jit(solution)/shard_map/psum | solution.py:100
  106.0 8.8 %collective-permute-start.6 = (bf16[1,45,256]{2,1,0:T(8,128)(2,1)S(1)}, bf16[1,45,256]{2,1,0:T(8,128)(2,1)S(1)}, u32[]{:S(2)}, u32[]{:S(2)}) collective-permute-start(bf16[1,45,256]{2,1,0:T(8,128)(2,1)S(1)} %get-tuple-element.35), channel_id=1, source_target_pairs={{8,0},{16,8},{24,16},{0,24},{9,1},{17,9},{25,17},{1,25},{10,2},{18... | collective-permute-start | bytes 69128 | tf_op jit(solution)/shard_map/ppermute | solution.py:17
  107.9 4.7 %collective-permute-start.5 = (bf16[1,45,256]{2,1,0:T(8,128)(2,1)S(1)}, bf16[1,45,256]{2,1,0:T(8,128)(2,1)S(1)}, u32[]{:S(2)}, u32[]{:S(2)}) collective-permute-start(bf16[1,45,256]{2,1,0:T(8,128)(2,1)S(1)} %get-tuple-element.36), channel_id=1, source_target_pairs={{0,8},{8,16},{16,24},{24,0},{1,9},{9,17},{17,25},{25,1},{2,10},{10... | collective-permute-start | bytes 69128 | tf_op jit(solution)/shard_map/ppermute | solution.py:15
  115.7 9.1 %collective-permute-start.7 = (bf16[92,1,256]{2,1,0:T(2,128)(2,1)}, bf16[92,1,256]{2,1,0:T(2,128)(2,1)}, u32[]{:S(2)}, u32[]{:S(2)}) collective-permute-start(bf16[92,1,256]{2,1,0:T(2,128)(2,1)} %get-tuple-element.31), channel_id=1, source_target_pairs={{0,1},{1,2},{2,3},{3,4},{4,5},{5,6},{6,7},{7,0},{8,9},{9,10},{10,1... | collective-permute-start | bytes 141320 | tf_op jit(solution)/shard_map/ppermute | solution.py:15
  115.7 9.1 %collective-permute-start.8 = (bf16[92,1,256]{2,1,0:T(2,128)(2,1)}, bf16[92,1,256]{2,1,0:T(2,128)(2,1)S(1)}, u32[]{:S(2)}, u32[]{:S(2)}) collective-permute-start(bf16[92,1,256]{2,1,0:T(2,128)(2,1)} %get-tuple-element.32), channel_id=1, source_target_pairs={{1,0},{2,1},{3,2},{4,3},{5,4},{6,5},{7,6},{0,7},{9,8},{10,9},{11,1... | collective-permute-start | bytes 141320 | tf_op jit(solution)/shard_map/ppermute | solution.py:17
  125.4 172.7 %collective-permute-start.9 = (bf16[2,47,256]{2,1,0:T(8,128)(2,1)S(1)}, bf16[2,47,256]{2,1,0:T(8,128)(2,1)S(1)}, u32[]{:S(2)}, u32[]{:S(2)}) collective-permute-start(bf16[2,47,256]{2,1,0:T(8,128)(2,1)S(1)} %fusion.57), channel_id=1, source_target_pairs={{0,4},{1,5},{2,6},{3,7},{4,0},{5,1},{6,2},{7,3},{8,12},{9,13},{10,... | collective-permute-start | bytes 144392 | tf_op jit(solution)/shard_map/ppermute | solution.py:27
  141.0 3.6 copy-start
  286.4 1.3 copy-start.7
  287.7 10.5 %copy-start.4 = (bf16[1,3,256,256]{3,2,1,0:T(8,128)(2,1)S(1)}, bf16[1,3,256,256]{3,2,1,0:T(8,128)(2,1)}, u32[]{:S(2)}) copy-start(bf16[1,3,256,256]{3,2,1,0:T(8,128)(2,1)} %get-tuple-element.40) | copy-start | bytes 1179652
  287.7 10.7 %copy-start.3 = (bf16[1,3,256,256]{3,2,1,0:T(8,128)(2,1)S(1)}, bf16[1,3,256,256]{3,2,1,0:T(8,128)(2,1)}, u32[]{:S(2)}) copy-start(bf16[1,3,256,256]{3,2,1,0:T(8,128)(2,1)} %get-tuple-element.39) | copy-start | bytes 1179652
  298.6 1.6 copy-start.6
Sparse Core Ops, SparseCore 0:
  105.2 171.7 all-gather.2
  286.5 71.1 all-reduce.1
